TPU v7x, 32 devices: a whole 2x2x4 slice. The times are simulated.
32 devices in a mesh: group: 4 (over x, core), replica: 8 (over z, y).
Axes of the slice: x: 2, y: 2, z: 4, core: 2. Of those that a mesh axis runs over, the one named last changes fastest.
Arguments:
- activations: float32 [16, 1024, 768], P('replica', 'group'), may hold values from -6 to 6
- out_grad: float32 [16, 1024, 768], P('replica', 'group'), may hold values from -6 to 6
- picture_ids: int32 [16, 1024], P('replica'), may hold values from -1 to 9, as said below
- ln1_gain: float32 [768], P('group'), may hold values from 0.5 to 1.5
- ln1_bias: float32 [768], P('group'), may hold values from -3 to 3
- w_query: float32 [768, 768], P(None, 'group'), may hold values from -0.3125 to 0.3125
- q_bias: float32 [768], P('group'), may hold values from -3 to 3
- w_key: float32 [768, 768], P(None, 'group'), may hold values from -0.3125 to 0.3125
- w_value: float32 [768, 768], P(None, 'group'), may hold values from -0.21875 to 0.21875
- v_bias: float32 [768], P('group'), may hold values from -3 to 3
- w_out: float32 [768, 768], P('group'), may hold values from -1.75 to 1.75
- out_bias: float32 [768], P('group'), may hold values from -3 to 3
- ln2_gain: float32 [768], P('group'), may hold values from 0.5 to 1.5
- ln2_bias: float32 [768], P('group'), may hold values from -3 to 3
- w_fc1: float32 [768, 3072], P(None, 'group'), may hold values from -0.21875 to 0.21875
- fc1_bias: float32 [3072], P('group'), may hold values from -3 to 3
- w_fc2: float32 [3072, 768], P('group'), may hold values from -0.109375 to 0.109375
- fc2_bias: float32 [768], P('group'), may hold values from -3 to 3
Outputs:
- output: float32 [16, 1024, 768], P('replica', 'group')
- grad_input: float32 [16, 1024, 768], P('replica', 'group')
- grad_ln1_gain: float32 [768], P('group')
- grad_ln1_bias: float32 [768], P('group')
- grad_w_query: float32 [768, 768], P(None, 'group')
- grad_q_bias: float32 [768], P('group')
- grad_w_key: float32 [768, 768], P(None, 'group')
- grad_w_value: float32 [768, 768], P(None, 'group')
- grad_v_bias: float32 [768], P('group')
- grad_w_out: float32 [768, 768], P('group')
- grad_out_bias: float32 [768], P('group')
- grad_ln2_gain: float32 [768], P('group')
- grad_ln2_bias: float32 [768], P('group')
- grad_w_fc1: float32 [768, 3072], P(None, 'group')
- grad_fc1_bias: float32 [3072], P('group')
- grad_w_fc2: float32 [3072, 768], P('group')
- grad_fc2_bias: float32 [768], P('group')
Inputs may be any that keep to these rules, and one draw needn't show every extreme that they name: `picture_ids`: each row holds whole pictures numbered 0, 1, 2 and so on from its start, each of 100 to 1024 patches, followed by padding marked -1.
All inputs are finite; a program needn't handle non-finite values.
Results may differ from a plain program's by a relative error of at most 0.04.
Values may be sent and summed in bfloat16 or wider, within the bound.
No kernel may reach another device: no remote copies, remote signals or barrier semaphores. Data moves between devices by JAX's collectives and lax.ppermute only.
A program may use at most 256 MiB of HBM per device.

v0:
```python
import jax
import jax.numpy as jnp
from jax import lax
from jax.sharding import PartitionSpec as P

HEADS = 12
HEAD_DIM = 64
EPS = 1e-06
MASKED = -1e30


def to_float(values):
    return values.astype(jnp.float32)


def normalize(values):
    centred = values - jnp.mean(values, axis=-1, keepdims=True)
    inverse = lax.rsqrt(jnp.mean(centred * centred, axis=-1, keepdims=True) + EPS)
    return (centred * inverse, inverse)


def norm_back(grad_hat, normed_hat, inverse):
    return inverse * (
        grad_hat
        - jnp.mean(grad_hat, axis=-1, keepdims=True)
        - normed_hat * jnp.mean(grad_hat * normed_hat, axis=-1, keepdims=True)
    )


def gelu_tanh(values):
    return jax.nn.gelu(values, approximate=True)


def heads_of(values):
    return values.reshape(values.shape[0], HEADS, HEAD_DIM)


def scores_of(query_rows, key_rows, query_ids, key_ids):
    raw_scores = jnp.einsum(
        "qhe,khe->hqk", heads_of(query_rows), heads_of(key_rows), preferred_element_type=jnp.float32
    ) * HEAD_DIM ** (-0.5)
    allowed = query_ids[:, None] == key_ids[None, :]
    return jnp.where(allowed[None], raw_scores, MASKED)


def attend_row(pieces):
    query_rows, key_rows, value_rows, query_ids, key_ids = pieces
    scores = scores_of(query_rows, key_rows, query_ids, key_ids)
    row_top = jnp.max(scores, axis=-1, keepdims=True)
    exponent = jnp.exp(scores - row_top)
    row_total = jnp.sum(exponent, axis=-1, keepdims=True)
    probability = (exponent / row_total).astype(jnp.bfloat16)
    attended = jnp.einsum(
        "hqk,khe->qhe", probability, heads_of(value_rows), preferred_element_type=jnp.float32
    )
    return (
        attended.reshape(query_rows.shape[0], -1).astype(jnp.bfloat16),
        (row_top + jnp.log(row_total))[..., 0],
    )


def attend_back(pieces):
    query_rows, key_rows, value_rows, query_ids, key_ids, logsum, grad_rows = pieces
    scores = scores_of(query_rows, key_rows, query_ids, key_ids)
    probability = jnp.exp(scores - logsum[..., None])
    grad_heads = heads_of(grad_rows)
    grad_value = jnp.einsum(
        "hqk,qhe->khe",
        probability.astype(jnp.bfloat16),
        grad_heads,
        preferred_element_type=jnp.float32,
    )
    grad_probs = jnp.einsum(
        "qhe,khe->hqk", grad_heads, heads_of(value_rows), preferred_element_type=jnp.float32
    )
    centre = jnp.sum(probability * grad_probs, axis=-1, keepdims=True)
    grad_scores = (probability * (grad_probs - centre)).astype(jnp.bfloat16)
    score_scale = HEAD_DIM ** (-0.5)
    grad_query = (
        jnp.einsum(
            "hqk,khe->qhe", grad_scores, heads_of(key_rows), preferred_element_type=jnp.float32
        )
        * score_scale
    )
    grad_key = (
        jnp.einsum(
            "hqk,qhe->khe", grad_scores, heads_of(query_rows), preferred_element_type=jnp.float32
        )
        * score_scale
    )
    query_count = query_rows.shape[0]
    key_count = key_rows.shape[0]
    return (
        grad_query.reshape(query_count, -1).astype(jnp.bfloat16),
        grad_key.reshape(key_count, -1),
        grad_value.reshape(key_count, -1),
    )


def per_device(
    activations,
    out_grad,
    picture_ids,
    ln1_gain,
    ln1_bias,
    w_query,
    q_bias,
    w_key,
    w_value,
    v_bias,
    w_out,
    out_bias,
    ln2_gain,
    ln2_bias,
    w_fc1,
    fc1_bias,
    w_fc2,
    fc2_bias,
):
    row_block, local_len, width = activations.shape
    row_total = row_block * local_len
    offset = lax.axis_index("group") * local_len
    own_ids = lax.dynamic_slice_in_dim(picture_ids, offset, local_len, 1)
    (
        query_full,
        key_full,
        value_full,
        out_full,
        gain_one,
        shift_one,
        bias_query,
        bias_value,
        bias_out,
        gain_two,
        shift_two,
        bias_fc2,
    ) = (
        lax.all_gather(w_query.astype(jnp.bfloat16), "group", axis=1, tiled=True),
        lax.all_gather(w_key.astype(jnp.bfloat16), "group", axis=1, tiled=True),
        lax.all_gather(w_value.astype(jnp.bfloat16), "group", axis=1, tiled=True),
        lax.all_gather(w_out.astype(jnp.bfloat16), "group", axis=0, tiled=True),
        lax.all_gather(ln1_gain.astype(jnp.bfloat16), "group", axis=0, tiled=True),
        lax.all_gather(ln1_bias.astype(jnp.bfloat16), "group", axis=0, tiled=True),
        lax.all_gather(q_bias.astype(jnp.bfloat16), "group", axis=0, tiled=True),
        lax.all_gather(v_bias.astype(jnp.bfloat16), "group", axis=0, tiled=True),
        lax.all_gather(out_bias.astype(jnp.bfloat16), "group", axis=0, tiled=True),
        lax.all_gather(ln2_gain.astype(jnp.bfloat16), "group", axis=0, tiled=True),
        lax.all_gather(ln2_bias.astype(jnp.bfloat16), "group", axis=0, tiled=True),
        lax.all_gather(fc2_bias.astype(jnp.bfloat16), "group", axis=0, tiled=True),
    )
    inputs = activations.reshape(row_total, width)
    hat_one, inverse_one = normalize(inputs)
    normed_one = (hat_one * to_float(gain_one) + to_float(shift_one)).astype(jnp.bfloat16)
    queries = (
        jnp.dot(normed_one, query_full, preferred_element_type=jnp.float32) + to_float(bias_query)
    ).astype(jnp.bfloat16)
    keys_new = jnp.dot(normed_one, key_full, preferred_element_type=jnp.float32).astype(
        jnp.bfloat16
    )
    values_new = (
        jnp.dot(normed_one, value_full, preferred_element_type=jnp.float32) + to_float(bias_value)
    ).astype(jnp.bfloat16)
    key_all, value_all = (
        lax.all_gather(keys_new.reshape(row_block, local_len, width), "group", axis=1, tiled=True),
        lax.all_gather(
            values_new.reshape(row_block, local_len, width), "group", axis=1, tiled=True
        ),
    )
    query_rows = queries.reshape(row_block, local_len, width)
    attended, logsum = lax.map(attend_row, (query_rows, key_all, value_all, own_ids, picture_ids))
    attended = attended.reshape(row_total, width)
    middle = inputs + (
        jnp.dot(attended, out_full, preferred_element_type=jnp.float32) + to_float(bias_out)
    )
    hat_two, inverse_two = normalize(middle)
    normed_two = (hat_two * to_float(gain_two) + to_float(shift_two)).astype(jnp.bfloat16)
    fc1_full, fc2_full, bias_fc1 = (
        lax.all_gather(w_fc1.astype(jnp.bfloat16), "group", axis=1, tiled=True),
        lax.all_gather(w_fc2.astype(jnp.bfloat16), "group", axis=0, tiled=True),
        lax.all_gather(fc1_bias.astype(jnp.bfloat16), "group", axis=0, tiled=True),
    )
    hidden = jnp.dot(normed_two, fc1_full, preferred_element_type=jnp.float32) + to_float(bias_fc1)
    gelu_value, gelu_pull = jax.vjp(gelu_tanh, hidden)
    activated = gelu_value.astype(jnp.bfloat16)
    mlp_output = jnp.dot(activated, fc2_full, preferred_element_type=jnp.float32)
    output = middle + (mlp_output + to_float(bias_fc2))
    valid_rows = (own_ids >= 0).astype(jnp.float32).reshape(row_total, 1)
    grad_out = out_grad.reshape(row_total, width) * valid_rows
    grad_mlp = grad_out.astype(jnp.bfloat16)
    grad_bias_fc2 = jnp.sum(to_float(grad_mlp), axis=0)
    grad_activated = jnp.dot(grad_mlp, fc2_full.T, preferred_element_type=jnp.float32)
    grad_fc2 = jnp.dot(activated.T, grad_mlp, preferred_element_type=jnp.float32)
    grad_hidden = gelu_pull(grad_activated)[0].astype(jnp.bfloat16)
    grad_fc1 = jnp.dot(normed_two.T, grad_hidden, preferred_element_type=jnp.float32)
    grad_bias_fc1 = jnp.sum(to_float(grad_hidden), axis=0)
    grad_normed_two = jnp.dot(grad_hidden, fc1_full.T, preferred_element_type=jnp.float32)
    grad_fc1, grad_fc2, grad_bias_fc1 = (
        lax.psum_scatter(
            grad_fc1.astype(jnp.bfloat16), "group", scatter_dimension=1, tiled=True
        ).astype(jnp.float32),
        lax.psum_scatter(
            grad_fc2.astype(jnp.bfloat16), "group", scatter_dimension=0, tiled=True
        ).astype(jnp.float32),
        lax.psum_scatter(
            grad_bias_fc1.astype(jnp.bfloat16), "group", scatter_dimension=0, tiled=True
        ).astype(jnp.float32),
    )
    grad_gain_two = jnp.sum(grad_normed_two * hat_two, axis=0)
    grad_shift_two = jnp.sum(grad_normed_two, axis=0)
    grad_middle = grad_out + norm_back(grad_normed_two * to_float(gain_two), hat_two, inverse_two)
    grad_branch = grad_middle.astype(jnp.bfloat16)
    grad_bias_out = jnp.sum(to_float(grad_branch), axis=0)
    grad_out_full = jnp.dot(attended.T, grad_branch, preferred_element_type=jnp.float32)
    grad_attended = jnp.dot(grad_branch, out_full.T, preferred_element_type=jnp.float32).astype(
        jnp.bfloat16
    )
    grad_att_rows = grad_attended.reshape(row_block, local_len, width)
    grad_queries, key_parts, value_parts = lax.map(
        attend_back, (query_rows, key_all, value_all, own_ids, picture_ids, logsum, grad_att_rows)
    )
    grad_keys, grad_values = (
        lax.psum_scatter(
            key_parts.astype(jnp.bfloat16), "group", scatter_dimension=1, tiled=True
        ).astype(jnp.float32),
        lax.psum_scatter(
            value_parts.astype(jnp.bfloat16), "group", scatter_dimension=1, tiled=True
        ).astype(jnp.float32),
    )
    grad_queries = grad_queries.reshape(row_total, width)
    grad_keys = grad_keys.reshape(row_total, width).astype(jnp.bfloat16)
    grad_values = grad_values.reshape(row_total, width).astype(jnp.bfloat16)
    grad_query_full = jnp.dot(normed_one.T, grad_queries, preferred_element_type=jnp.float32)
    grad_key_full = jnp.dot(normed_one.T, grad_keys, preferred_element_type=jnp.float32)
    grad_value_full = jnp.dot(normed_one.T, grad_values, preferred_element_type=jnp.float32)
    grad_bias_query = jnp.sum(to_float(grad_queries), axis=0)
    grad_bias_value = jnp.sum(to_float(grad_values), axis=0)
    grad_normed_one = jnp.dot(grad_queries, query_full.T, preferred_element_type=jnp.float32)
    grad_normed_one = grad_normed_one + jnp.dot(
        grad_keys, key_full.T, preferred_element_type=jnp.float32
    )
    grad_normed_one = grad_normed_one + jnp.dot(
        grad_values, value_full.T, preferred_element_type=jnp.float32
    )
    grad_gain_one = jnp.sum(grad_normed_one * hat_one, axis=0)
    grad_shift_one = jnp.sum(grad_normed_one, axis=0)
    grad_input = grad_middle + norm_back(grad_normed_one * to_float(gain_one), hat_one, inverse_one)
    (
        grad_query_full,
        grad_key_full,
        grad_value_full,
        grad_out_full,
        grad_gain_one,
        grad_shift_one,
        grad_bias_query,
        grad_bias_value,
        grad_bias_out,
        grad_gain_two,
        grad_shift_two,
        grad_bias_fc2,
    ) = (
        lax.psum_scatter(
            grad_query_full.astype(jnp.bfloat16), "group", scatter_dimension=1, tiled=True
        ).astype(jnp.float32),
        lax.psum_scatter(
            grad_key_full.astype(jnp.bfloat16), "group", scatter_dimension=1, tiled=True
        ).astype(jnp.float32),
        lax.psum_scatter(
            grad_value_full.astype(jnp.bfloat16), "group", scatter_dimension=1, tiled=True
        ).astype(jnp.float32),
        lax.psum_scatter(
            grad_out_full.astype(jnp.bfloat16), "group", scatter_dimension=0, tiled=True
        ).astype(jnp.float32),
        lax.psum_scatter(
            grad_gain_one.astype(jnp.bfloat16), "group", scatter_dimension=0, tiled=True
        ).astype(jnp.float32),
        lax.psum_scatter(
            grad_shift_one.astype(jnp.bfloat16), "group", scatter_dimension=0, tiled=True
        ).astype(jnp.float32),
        lax.psum_scatter(
            grad_bias_query.astype(jnp.bfloat16), "group", scatter_dimension=0, tiled=True
        ).astype(jnp.float32),
        lax.psum_scatter(
            grad_bias_value.astype(jnp.bfloat16), "group", scatter_dimension=0, tiled=True
        ).astype(jnp.float32),
        lax.psum_scatter(
            grad_bias_out.astype(jnp.bfloat16), "group", scatter_dimension=0, tiled=True
        ).astype(jnp.float32),
        lax.psum_scatter(
            grad_gain_two.astype(jnp.bfloat16), "group", scatter_dimension=0, tiled=True
        ).astype(jnp.float32),
        lax.psum_scatter(
            grad_shift_two.astype(jnp.bfloat16), "group", scatter_dimension=0, tiled=True
        ).astype(jnp.float32),
        lax.psum_scatter(
            grad_bias_fc2.astype(jnp.bfloat16), "group", scatter_dimension=0, tiled=True
        ).astype(jnp.float32),
    )
    (
        grad_query_full,
        grad_key_full,
        grad_value_full,
        grad_out_full,
        grad_gain_one,
        grad_shift_one,
        grad_bias_query,
        grad_bias_value,
        grad_bias_out,
        grad_gain_two,
        grad_shift_two,
        grad_bias_fc2,
        grad_fc1,
        grad_fc2,
        grad_bias_fc1,
    ) = lax.psum(
        (
            grad_query_full,
            grad_key_full,
            grad_value_full,
            grad_out_full,
            grad_gain_one,
            grad_shift_one,
            grad_bias_query,
            grad_bias_value,
            grad_bias_out,
            grad_gain_two,
            grad_shift_two,
            grad_bias_fc2,
            grad_fc1,
            grad_fc2,
            grad_bias_fc1,
        ),
        "replica",
    )
    return (
        output.reshape(row_block, local_len, width),
        grad_input.reshape(row_block, local_len, width),
        grad_gain_one,
        grad_shift_one,
        grad_query_full,
        grad_bias_query,
        grad_key_full,
        grad_value_full,
        grad_bias_value,
        grad_out_full,
        grad_bias_out,
        grad_gain_two,
        grad_shift_two,
        grad_fc1,
        grad_bias_fc1,
        grad_fc2,
        grad_bias_fc2,
    )


def solution(mesh):
    placed = (
        P("replica", "group", None),
        P("replica", "group", None),
        P("replica", None),
        P("group"),
        P("group"),
        P(None, "group"),
        P("group"),
        P(None, "group"),
        P(None, "group"),
        P("group"),
        P("group", None),
        P("group"),
        P("group"),
        P("group"),
        P(None, "group"),
        P("group"),
        P("group", None),
        P("group"),
    )
    return jax.shard_map(
        per_device,
        mesh=mesh,
        in_specs=placed,
        out_specs=(
            P("replica", "group", None),
            P("replica", "group", None),
            P("group"),
            P("group"),
            P(None, "group"),
            P("group"),
            P(None, "group"),
            P(None, "group"),
            P("group"),
            P("group", None),
            P("group"),
            P("group"),
            P("group"),
            P(None, "group"),
            P("group"),
            P("group", None),
            P("group"),
        ),
        check_vma=False,
    )
```

profile of v0, /device:TPU:0, one launch (start us, length us, event | category | flops | bytes accessed | tf_op | source)
XLA Modules:
  0.0 935.0 jit_solution(2342156140588591705)
XLA Ops:
  7.3 1.9 convert_element_type.265
  13.8 13.2 %all-reduce.19 = (bf16[768]{0:T(1024)(128)(2,1)S(1)}, bf16[768]{0:T(1024)(128)(2,1)S(1)}, bf16[768]{0:T(1024)(128)(2,1)S(1)}, bf16[768]{0:T(1024)(128)(2,1)S(1)}...) all-reduce(bf16[768]{0:T(1024)(128)(2,1)S(1)} %dynamic-update-slice, ...), channel_id=1, replica_groups=mesh['group'=4,'replica'=8] {'group'}, use_global_device_ids=true, to_apply=%add.1 | all-reduce | flops 5376 | bytes 21504
  28.7 1.9 all-gather.10.cloned.1.call-done
  30.6 2.1 add_convert_fusion.3
  33.9 16.3 %all-gather.16.cloned.1.call-done = bf16[768,768]{0,1:T(8,128)(2,1)} async-done(((bf16[768,192]{0,1:T(8,128)(2,1)}), bf16[768,768]{0,1:T(8,128)(2,1)}) %all-gather.16.cloned.1.call-update) | async-done | bytes 1179664 | tf_op jit(solution)/shard_map/all_gather | solution.py:139
  50.2 2.1 convolution_convert_fusion.4
  54.4 2.8 convert_element_type.283
  57.3 3.0 convert_element_type.287
  62.3 5.2 all-gather
  69.9 2.3 add_convert_fusion.2
  72.5 28.4 %all-gather.12.cloned.1.call-done = bf16[2,1024,768]{1,2,0:T(8,128)(2,1)} async-done(((bf16[2,256,768]{1,2,0:T(8,128)(2,1)}), bf16[2,1024,768]{1,2,0:T(8,128)(2,1)}) %all-gather.12.cloned.1.call-update) | async-done | bytes 3145744 | tf_op jit(solution)/shard_map/all_gather | solution.py:165
  100.9 30.4 %all-gather.18.cloned.1.call-done = bf16[2,1024,768]{1,2,0:T(8,128)(2,1)} async-done(((bf16[2,256,768]{1,2,0:T(8,128)(2,1)}), bf16[2,1024,768]{1,2,0:T(8,128)(2,1)}) %all-gather.18.cloned.1.call-update) | async-done | bytes 3145744 | tf_op jit(solution)/shard_map/all_gather | solution.py:164
  131.2 29.5 %while.26 = (s32[]{:T(128)}, bf16[2,256,768]{2,1,0:T(8,128)(2,1)}, f32[2,12,256]{2,1,0:T(8,128)}, bf16[2,1024,768]{1,2,0:T(8,128)(2,1)}, s32[2,256]{1,0:T(2,128)...) while((s32[]{:T(128)}, bf16[2,256,768]{2,1,0:T(8,128)(2,1)}, ...), condition=%wide.region_5.6_spmd, body=%wide.region_2.5_spmd.sunk | while | flops 843510784 | bytes 51499116 | solution.py:170
  132.3 2.2 constant_dynamic-slice_fusion.23
  134.6 2.3 fusion.100
  136.9 3.6 fusion.101
  141.1 3.9 fusion.102
  147.0 2.2 constant_dynamic-slice_fusion.23
  149.2 2.3 fusion.100
  151.5 3.6 fusion.101
  155.8 3.9 fusion.102
  160.7 2.6 fusion.32
  164.8 25.6 %all-gather.22.cloned.1.call-done = bf16[768,3072]{1,0:T(8,128)(2,1)} async-done(((bf16[768,768]{1,0:T(8,128)(2,1)}), bf16[768,3072]{1,0:T(8,128)(2,1)}) %all-gather.22.cloned.1.call-update) | async-done | bytes 4718608 | tf_op jit(solution)/shard_map/all_gather | solution.py:178
  190.4 8.2 fusion.28
  198.6 31.4 %all-gather.24.cloned.1.call-done = bf16[3072,768]{1,0:T(8,128)(2,1)} async-done(((bf16[768,768]{1,0:T(8,128)(2,1)}), bf16[3072,768]{1,0:T(8,128)(2,1)}) %all-gather.24.cloned.1.call-update) | async-done | bytes 4718608 | tf_op jit(solution)/shard_map/all_gather | solution.py:179
  230.0 9.8 %fusion.29 = (bf16[3072]{0:T(1024)(128)(2,1)}, bf16[512,3072]{1,0:T(8,128)(2,1)S(1)}) fusion(f32[512,3072]{1,0:T(8,128)} %fusion.28, f32[3072]{0:T(1024)S(1)} %bitcast.212, bf16[512,768]{1,0:T(8,128)(2,1)S(1)} %copy-done.22, bf16[3072,768]{1,0:T(8,128)(2,1)} %all-gather.24.cloned.1.call-done), kind=kOutput, calls=%fused_computation.108 | convolution fusion | flops 2450519040 | bytes 14960640 | tf_op jit(solution)/shard_map/dot_general | solution.py:191
  239.8 3.5 multiply_reduce_fusion.1
  245.7 109.7 %while.27 = (s32[]{:T(128)}, bf16[2,256,768]{1,2,0:T(8,128)(2,1)}, bf16[2,1024,768]{2,1,0:T(8,128)(2,1)}, bf16[2,1024,768]{2,1,0:T(8,128)(2,1)}, bf16[2,1024,768...) while((s32[]{:T(128)}, bf16[2,256,768]{1,2,0:T(8,128)(2,1)}, ...), condition=%wide.region_12.13_spmd, body=%wide.region_10.12_spmd.sunk | while | flops 2062676992 | bytes 238015056 | solution.py:218
  246.1 2.1 constant_dynamic-slice_fusion.27
  248.3 6.4 fusion.113
  258.3 11.5 %multiply_reduce_fusion.10 = (f32[12,256]{1,0:T(8,128)S(1)}, f32[12,256,1024]{2,1,0:T(8,128)}) fusion(f32[12,256,1024]{2,1,0:T(8,128)} %fusion.113, f32[12,256]{1,0:T(8,128)S(1)} %dynamic-slice_bitcast_fusion.2, pred[256,1024]{1,0:T(8,128)(4,1)S(1)} %broadcast_compare_fusion.5, bf16[256,12,64]{0,2,1:T(8,128)(2,1)S(1)} %bitcast.188, ...), kind=kOutput, calls=%fused_computation.18.clone.1 | convolution fusion | flops 418378752 | bytes 27418624 | tf_op jit(solution)/shard_map/while/body/eval_jaxpr/qhe,khe->hqk/dot_general | solution.py:73
  270.9 6.7 multiply_convert_fusion.6
  281.8 9.0 fusion.115
  290.8 2.7 copy.97
  293.5 3.5 constant_dynamic-update-slice_fusion.9
  297.9 2.0 fusion.114
  300.8 2.1 constant_dynamic-slice_fusion.27
  302.9 6.4 fusion.113
  313.0 11.5 %multiply_reduce_fusion.10 = (f32[12,256]{1,0:T(8,128)S(1)}, f32[12,256,1024]{2,1,0:T(8,128)}) fusion(f32[12,256,1024]{2,1,0:T(8,128)} %fusion.113, f32[12,256]{1,0:T(8,128)S(1)} %dynamic-slice_bitcast_fusion.2, pred[256,1024]{1,0:T(8,128)(4,1)S(1)} %broadcast_compare_fusion.5, bf16[256,12,64]{0,2,1:T(8,128)(2,1)S(1)} %bitcast.188, ...), kind=kOutput, calls=%fused_computation.18.clone.1 | convolution fusion | flops 418378752 | bytes 27418624 | tf_op jit(solution)/shard_map/while/body/eval_jaxpr/qhe,khe->hqk/dot_general | solution.py:73
  325.6 6.7 multiply_convert_fusion.6
  336.5 9.0 fusion.115
  345.5 2.7 copy.97
  348.2 3.4 constant_dynamic-update-slice_fusion.9
  352.6 2.0 fusion.114
  358.3 3.0 bitcast_convert_fusion.2
  361.4 2.9 convolution_convert_fusion.2
  364.4 29.1 %reduce-scatter.9.cloned.1.call-done = bf16[2,256,768]{2,1,0:T(8,128)(2,1)} async-done(((bf16[2,1024,768]{2,1,0:T(8,128)(2,1)}), bf16[2,256,768]{2,1,0:T(8,128)(2,1)}) %reduce-scatter.9.cloned.1.call-update) | async-done | bytes 786448 | tf_op jit(solution)/shard_map/reduce_scatter | solution.py:222
  393.6 3.2 bitcast_convert_fusion.1
  396.9 37.2 %reduce-scatter.11.cloned.1.call-done = bf16[2,256,768]{2,1,0:T(8,128)(2,1)} async-done(((bf16[2,1024,768]{2,1,0:T(8,128)(2,1)}), bf16[2,256,768]{2,1,0:T(8,128)(2,1)}) %reduce-scatter.11.cloned.1.call-update) | async-done | bytes 786448 | tf_op jit(solution)/shard_map/reduce_scatter | solution.py:225
  434.1 3.3 bitcast_convert_fusion
  437.5 7.4 convolution_convert_fusion.1
  445.6 8.9 convolution_convert_fusion
  458.3 2.3 copy.57
  461.9 3.4 fusion.34
  465.4 26.0 %reduce-scatter.19.cloned.1.call-done = bf16[192,768]{1,0:T(8,128)(2,1)} async-done(((bf16[768,768]{1,0:T(8,128)(2,1)}), bf16[192,768]{1,0:T(8,128)(2,1)}) %reduce-scatter.19.cloned.1.call-update) | async-done | bytes 294928 | tf_op jit(solution)/shard_map/reduce_scatter | solution.py:270
  492.7 2.4 fusion.35
  495.3 2.4 multiply_reduce_fusion.2
  497.7 10.3 %all-reduce.18 = (bf16[768]{0:T(1024)(128)(2,1)S(1)}, bf16[768]{0:T(1024)(128)(2,1)S(1)}, bf16[768]{0:T(1024)(128)(2,1)S(1)}, bf16[768]{0:T(1024)(128)(2,1)S(1)}...) all-reduce(bf16[768]{0:T(1024)(128)(2,1)S(1)} %dynamic-update-slice, ...), channel_id=1, replica_groups=mesh['group'=4,'replica'=8] {'group'}, use_global_device_ids=true, to_apply=%add.7 | all-reduce | flops 9984 | bytes 39936
  508.6 3.2 multiply_add_fusion
  511.8 9.3 add_add_fusion.1
  521.1 27.5 %reduce-scatter.17.cloned.1.call-done = bf16[768,192]{0,1:T(8,128)(2,1)} async-done(((bf16[768,768]{0,1:T(8,128)(2,1)}), bf16[768,192]{0,1:T(8,128)(2,1)}) %reduce-scatter.17.cloned.1.call-update) | async-done | bytes 294928 | tf_op jit(solution)/shard_map/reduce_scatter | solution.py:267
  548.6 50.2 %reduce-scatter.21.cloned.1.call-done = bf16[768,768]{1,0:T(8,128)(2,1)} async-done(((bf16[768,3072]{1,0:T(8,128)(2,1)}), bf16[768,768]{1,0:T(8,128)(2,1)}) %reduce-scatter.21.cloned.1.call-update) | async-done | bytes 1179664 | tf_op jit(solution)/shard_map/reduce_scatter | solution.py:198
  598.8 50.5 %reduce-scatter.23.cloned.1.call-done = bf16[768,768]{1,0:T(8,128)(2,1)} async-done(((bf16[3072,768]{1,0:T(8,128)(2,1)}), bf16[768,768]{1,0:T(8,128)(2,1)}) %reduce-scatter.23.cloned.1.call-update) | async-done | bytes 1179664 | tf_op jit(solution)/shard_map/reduce_scatter | solution.py:201
  649.3 279.1 %all-reduce.21 = (f32[192]{0:T(256)}, f32[192]{0:T(256)}, f32[768,192]{0,1:T(8,128)}, f32[192]{0:T(256)}, f32[768,192]{0,1:T(8,128)}, /*index=5*/f32[768,192]{0,...) all-reduce(f32[192]{0:T(256)S(1)} %dynamic-slice_convert_fusion.8, ...), channel_id=1, replica_groups=mesh['group'=4,'replica'=8] {'replica'}, use_global_device_ids=true, to_apply=%region_19.20 | all-reduce | flops 1771776 | bytes 10635264 | tf_op jit(solution)/shard_map/psum | solution.py:314
  (335 shorter events, 53.1 us)
Async XLA Ops:
  7.2 2.9 copy-start.26
  7.2 3.7 copy-start.64
  7.2 3.8 copy-start.65
  7.2 3.8 copy-start.66
  7.2 3.8 copy-start.67
  7.3 3.8 copy-start.68
  7.3 3.8 copy-start.69
  7.3 3.8 copy-start.70
  7.3 23.3 %all-gather.10.cloned.1.call-start = ((), (), s32[]{:S(2)}) async-start(), calls=%async_computation.8 | async-start | bytes 1474560 | tf_op jit(solution)/shard_map/all_gather | solution.py:140
  9.2 17.8 %copy-start.5 = (f32[2,256,768]{2,1,0:T(8,128)S(1)}, f32[2,256,768]{2,1,0:T(8,128)}, u32[]{:S(2)}) copy-start(f32[2,256,768]{2,1,0:T(8,128)} %param.22) | copy-start | bytes 4718596
  9.2 41.0 %all-gather.16.cloned.1.call-start = ((), (), s32[]{:S(2)}) async-start(), calls=%async_computation.11 | async-start | bytes 1474560 | tf_op jit(solution)/shard_map/all_gather | solution.py:139
  10.1 59.8 %all-gather.14.cloned.1.call-start = ((), (), s32[]{:S(2)}) async-start(), calls=%async_computation.10 | async-start | bytes 1474560 | tf_op jit(solution)/shard_map/all_gather | solution.py:138
  10.9 90.0 %all-gather.12.cloned.1.call-start = ((), (), s32[]{:S(2)}) async-start(), calls=%async_computation.9 | async-start | bytes 3932160 | tf_op jit(solution)/shard_map/all_gather | solution.py:165
  28.7 21.5 %copy-start.23 = (bf16[512,768]{1,0:T(8,128)(2,1)}, bf16[512,768]{1,0:T(8,128)(2,1)S(1)}, u32[]{:S(2)}) copy-start(bf16[512,768]{1,0:T(8,128)(2,1)S(1)} %add_convert_fusion.4) | copy-start | bytes 2359300
  33.8 97.4 %all-gather.18.cloned.1.call-start = ((), (), s32[]{:S(2)}) async-start(), calls=%async_computation.12 | async-start | bytes 3932160 | tf_op jit(solution)/shard_map/all_gather | solution.py:164
  53.5 107.2 %all-gather.20.cloned.1.call-start = ((), (), s32[]{:S(2)}) async-start(), calls=%async_computation.13 | async-start | bytes 1474560 | tf_op jit(solution)/shard_map/all_gather | solution.py:141
  54.3 136.0 %all-gather.22.cloned.1.call-start = ((), (), s32[]{:S(2)}) async-start(), calls=%async_computation.14 | async-start | bytes 5898240 | tf_op jit(solution)/shard_map/all_gather | solution.py:178
  57.2 5.1 copy-start.56
  57.2 10.9 %copy-start.12 = (f32[2,256,768]{2,1,0:T(8,128)S(1)}, f32[2,256,768]{2,1,0:T(8,128)}, u32[]{:S(2)}) copy-start(f32[2,256,768]{2,1,0:T(8,128)} %param.23) | copy-start | bytes 4718596
  57.2 172.7 %all-gather.24.cloned.1.call-start = ((), (), s32[]{:S(2)}) async-start(), calls=%async_computation.15 | async-start | bytes 5898240 | tf_op jit(solution)/shard_map/all_gather | solution.py:179
  60.3 333.3 %reduce-scatter.9.cloned.1.call-start = ((), (), s32[]{:S(2)}) async-start(), calls=%async_computation.16 | async-start | bytes 3932160 | tf_op jit(solution)/shard_map/reduce_scatter | solution.py:222
  61.0 182.3 %copy-start.46 = (f32[768]{0:T(1024)}, f32[768]{0:T(1024)S(1)}, u32[]{:S(2)}) copy-start(f32[768]{0:T(1024)S(1)} %convert_element_type.279) | copy-start | bytes 9220
  61.0 129.4 %copy-start.57 = (f32[768]{0:T(1024)}, f32[768]{0:T(1024)S(1)}, u32[]{:S(2)}) copy-start(f32[768]{0:T(1024)S(1)} %convert_element_type.281) | copy-start | bytes 9220
  62.3 6.9 copy-start.44
  163.3 80.0 %copy-start.42 = (f32[512]{0:T(512)}, f32[512]{0:T(512)S(1)}, u32[]{:S(2)}) copy-start(f32[512]{0:T(512)S(1)} %broadcast_multiply_fusion.4) | copy-start | bytes 6148
  164.8 78.5 %copy-start.53 = (f32[512]{0:T(512)}, f32[512]{0:T(512)S(1)}, u32[]{:S(2)}) copy-start(f32[512]{0:T(512)S(1)} %add_rsqrt_fusion) | copy-start | bytes 6148
  164.8 65.2 %copy-start.22 = (bf16[512,768]{1,0:T(8,128)(2,1)S(1)}, bf16[512,768]{1,0:T(8,128)(2,1)}, u32[]{:S(2)}) copy-start(bf16[512,768]{1,0:T(8,128)(2,1)} %fusion.21) | copy-start | bytes 2359300
  164.8 65.2 %copy-start.48 = (f32[4,1,768]{2,1,0:T(1,128)S(1)}, f32[4,1,768]{2,1,0:T(1,128)}, u32[]{:S(2)}) copy-start(f32[4,1,768]{2,1,0:T(1,128)} %convert_element_type.326) | copy-start | bytes 36868
  230.0 9.8 %copy-start.15 = (f32[512,768]{1,0:T(8,128)S(1)}, f32[512,768]{1,0:T(8,128)}, u32[]{:S(2)}) copy-start(f32[512,768]{1,0:T(8,128)} %copy-done.14) | copy-start | bytes 4718596
  230.0 9.8 %copy-start.62 = (bf16[768,3072]{1,0:T(8,128)(2,1)S(1)}, bf16[768,3072]{1,0:T(8,128)(2,1)}, u32[]{:S(2)}) copy-start(bf16[768,3072]{1,0:T(8,128)(2,1)} %all-gather.22.cloned.1.call-done) | copy-start | bytes 14155780
  239.7 3.6 copy-start.72
  239.7 3.6 copy-start.13
  239.7 3.6 copy-start.45
  246.1 9.3 copy-start.32
  246.1 10.3 %copy-start.17 = (bf16[2,256,768]{2,1,0:T(8,128)(2,1)}, bf16[2,256,768]{2,1,0:T(8,128)(2,1)S(1)}, u32[]{:S(2)}) copy-start(bf16[2,256,768]{2,1,0:T(8,128)(2,1)S(1)} %get-tuple-element.477) | copy-start | bytes 2359300 | tf_op jit(solution)/shard_map/while
  255.6 14.3 %copy-start.3 = (pred[256,1024]{1,0:T(8,128)(4,1)}, pred[256,1024]{1,0:T(8,128)(4,1)S(1)}, u32[]{:S(2)}) copy-start(pred[256,1024]{1,0:T(8,128)(4,1)S(1)} %broadcast_compare_fusion.5) | copy-start | bytes 786436 | tf_op jit(solution)/shard_map/while
  258.3 11.6 %slice-start = ((s8[12582912]{0:T(1024)(128)(4,1)}), s8[4194304]{0:T(1024)(128)(4,1)S(1)}, s32[]{:S(2)}) async-start(s8[12582912]{0:T(1024)(128)(4,1)} %bitcast.175), calls=%async_computation.24 | async-start | bytes 8388608 | tf_op jit(solution)/shard_map/while
  258.3 11.6 %slice-start.1 = ((s8[12582912]{0:T(1024)(128)(4,1)}), s8[4194304]{0:T(1024)(128)(4,1)S(1)}, s32[]{:S(2)}) async-start(s8[12582912]{0:T(1024)(128)(4,1)} %bitcast.175), calls=%async_computation.25 | async-start | bytes 8388608 | tf_op jit(solution)/shard_map/while
  258.3 12.6 %slice-start.2 = ((s8[12582912]{0:T(1024)(128)(4,1)}), s8[4194304]{0:T(1024)(128)(4,1)S(1)}, s32[]{:S(2)}) async-start(s8[12582912]{0:T(1024)(128)(4,1)} %bitcast.175), calls=%async_computation.26 | async-start | bytes 8388608 | tf_op jit(solution)/shard_map/while
  293.5 4.4 copy-start.1
  297.9 2.8 copy-start.18
  297.9 2.8 copy-start.33
  300.8 9.3 copy-start.32
  300.8 10.3 %copy-start.17 = (bf16[2,256,768]{2,1,0:T(8,128)(2,1)}, bf16[2,256,768]{2,1,0:T(8,128)(2,1)S(1)}, u32[]{:S(2)}) copy-start(bf16[2,256,768]{2,1,0:T(8,128)(2,1)S(1)} %get-tuple-element.477) | copy-start | bytes 2359300 | tf_op jit(solution)/shard_map/while
  310.3 14.3 %copy-start.3 = (pred[256,1024]{1,0:T(8,128)(4,1)}, pred[256,1024]{1,0:T(8,128)(4,1)S(1)}, u32[]{:S(2)}) copy-start(pred[256,1024]{1,0:T(8,128)(4,1)S(1)} %broadcast_compare_fusion.5) | copy-start | bytes 786436 | tf_op jit(solution)/shard_map/while
  313.0 11.6 %slice-start = ((s8[12582912]{0:T(1024)(128)(4,1)}), s8[4194304]{0:T(1024)(128)(4,1)S(1)}, s32[]{:S(2)}) async-start(s8[12582912]{0:T(1024)(128)(4,1)} %bitcast.175), calls=%async_computation.24 | async-start | bytes 8388608 | tf_op jit(solution)/shard_map/while
  313.0 11.6 %slice-start.1 = ((s8[12582912]{0:T(1024)(128)(4,1)}), s8[4194304]{0:T(1024)(128)(4,1)S(1)}, s32[]{:S(2)}) async-start(s8[12582912]{0:T(1024)(128)(4,1)} %bitcast.175), calls=%async_computation.25 | async-start | bytes 8388608 | tf_op jit(solution)/shard_map/while
  313.0 12.6 %slice-start.2 = ((s8[12582912]{0:T(1024)(128)(4,1)}), s8[4194304]{0:T(1024)(128)(4,1)S(1)}, s32[]{:S(2)}) async-start(s8[12582912]{0:T(1024)(128)(4,1)} %bitcast.175), calls=%async_computation.26 | async-start | bytes 8388608 | tf_op jit(solution)/shard_map/while
  348.2 4.4 copy-start.1
  355.4 78.6 %reduce-scatter.11.cloned.1.call-start = ((), (), s32[]{:S(2)}) async-start(), calls=%async_computation.17 | async-start | bytes 3932160 | tf_op jit(solution)/shard_map/reduce_scatter | solution.py:225
  356.0 109.3 %reduce-scatter.13.cloned.1.call-start = ((), (), s32[]{:S(2)}) async-start(), calls=%async_computation.18 | async-start | bytes 1474560 | tf_op jit(solution)/shard_map/reduce_scatter | solution.py:261
  358.3 3.1 copy-start.11
  361.4 130.0 %reduce-scatter.19.cloned.1.call-start = ((), (), s32[]{:S(2)}) async-start(), calls=%async_computation.21 | async-start | bytes 1474560 | tf_op jit(solution)/shard_map/reduce_scatter | solution.py:270
  364.4 156.7 %reduce-scatter.15.cloned.1.call-start = ((), (), s32[]{:S(2)}) async-start(), calls=%async_computation.19 | async-start | bytes 1474560 | tf_op jit(solution)/shard_map/reduce_scatter | solution.py:264
  396.8 40.6 %copy-start.43 = (f32[512]{0:T(512)S(1)}, f32[512]{0:T(512)}, u32[]{:S(2)}) copy-start(f32[512]{0:T(512)} %copy-done.42) | copy-start | bytes 6148
  396.8 40.6 %copy-start.47 = (f32[768]{0:T(1024)S(1)}, f32[768]{0:T(1024)}, u32[]{:S(2)}) copy-start(f32[768]{0:T(1024)} %copy-done.46) | copy-start | bytes 9220
  396.8 40.6 %copy-start.54 = (f32[512]{0:T(512)S(1)}, f32[512]{0:T(512)}, u32[]{:S(2)}) copy-start(f32[512]{0:T(512)} %copy-done.53) | copy-start | bytes 6148
  396.8 40.6 %copy-start.58 = (f32[768]{0:T(1024)S(1)}, f32[768]{0:T(1024)}, u32[]{:S(2)}) copy-start(f32[768]{0:T(1024)} %copy-done.57) | copy-start | bytes 9220
  396.8 151.8 %reduce-scatter.17.cloned.1.call-start = ((), (), s32[]{:S(2)}) async-start(), calls=%async_computation.20 | async-start | bytes 1474560 | tf_op jit(solution)/shard_map/reduce_scatter | solution.py:267
  437.4 161.5 %reduce-scatter.21.cloned.1.call-start = ((), (), s32[]{:S(2)}) async-start(), calls=%async_computation.22 | async-start | bytes 5898240 | tf_op jit(solution)/shard_map/reduce_scatter | solution.py:198
  444.9 204.4 %reduce-scatter.23.cloned.1.call-start = ((), (), s32[]{:S(2)}) async-start(), calls=%async_computation.23 | async-start | bytes 5898240 | tf_op jit(solution)/shard_map/reduce_scatter | solution.py:201
  508.6 3.2 copy-start.16
  511.8 137.5 %copy-start.28 = (bf16[768,192]{0,1:T(8,128)(2,1)S(1)}, bf16[768,192]{0,1:T(8,128)(2,1)}, u32[]{:S(2)}) copy-start(bf16[768,192]{0,1:T(8,128)(2,1)} %reduce-scatter.13.cloned.1.call-done) | copy-start | bytes 884740
  511.8 137.5 %copy-start.29 = (bf16[192,768]{1,0:T(8,128)(2,1)S(1)}, bf16[192,768]{1,0:T(8,128)(2,1)}, u32[]{:S(2)}) copy-start(bf16[192,768]{1,0:T(8,128)(2,1)} %reduce-scatter.19.cloned.1.call-done) | copy-start | bytes 884740
  (43 other events, 79.7 us)
Sparse Core Ops, SparseCore 0:
  10.3 20.2 all-gather.9
  32.7 17.4 all-gather.15
  52.3 17.5 all-gather.13
  71.9 28.9 all-gather.11
  102.2 28.9 all-gather.17
  133.2 17.4 all-gather.19
  152.8 37.4 all-gather.21
  192.5 37.4 all-gather.23
  355.6 37.9 reduce-scatter.8
  396.1 37.9 reduce-scatter.10
  437.2 25.7 reduce-scatter.12
  465.6 25.7 reduce-scatter.18
  494.5 25.7 reduce-scatter.14
  522.8 25.7 reduce-scatter.16
  551.0 47.8 reduce-scatter.20
  601.4 47.8 reduce-scatter.22
where the time goes:
time: 942 us; the launch traced here: 935 us
  waiting for transfers between devices  356 us (38%)
  blocking collectives  308 us (33%)
  matrix products  151 us (16%)
  local copies, waits for them, and re-layouts  54.9 us (6%)
  other arithmetic  47.5 us (5%)
  between operations  17 us (2%)
    psum x1, blocking collectives, per_device(): lax.psum((grad_query_full, grad_key_full, grad_value_full, grad_out_full,...  279 us
    reduce_scatter x1, waiting for transfers between devices, per_device(): lax.psum_scatter(grad_fc2.astype(jnp.bfloat16), 'group', scatter_dimensio...  50.5 us
    reduce_scatter x1, waiting for transfers between devices, per_device(): lax.psum_scatter(grad_fc1.astype(jnp.bfloat16), 'group', scatter_dimensio...  50.2 us
    reduce_scatter x1, waiting for transfers between devices, per_device(): lax.psum_scatter(value_parts.astype(jnp.bfloat16), 'group', scatter_dimen...  37.2 us
    all_gather x1, waiting for transfers between devices, per_device(): lax.all_gather(w_fc2.astype(jnp.bfloat16), 'group', axis=0, tiled=True)  31.4 us
    all_gather x1, waiting for transfers between devices, per_device(): lax.all_gather(keys_new.reshape(row_block, local_len, width), 'group', ax...  30.4 us
    reduce_scatter x1, waiting for transfers between devices, per_device(): lax.psum_scatter(key_parts.astype(jnp.bfloat16), 'group', scatter_dimensi...  29.1 us
    all_gather x1, waiting for transfers between devices, per_device(): lax.all_gather(values_new.reshape(row_block, local_len, width), 'group',...  28.4 us
  transfers between devices with their start and end apart: 16, of which 13 were waited for; matrix products, arithmetic and copies ran while one was open for 13% of the time, Pallas kernels for 0%

commit v1 on v0

--- a/solution.py
+++ b/solution.py
@@ -117,6 +117,32 @@
     w_fc2,
     fc2_bias,
 ):
+
+    def review_pieces_all_all(local_x):
+        comm_axis = "group"
+        moved = jax.lax.axis_size(comm_axis)
+        value_now, piece_out, g_now = (moved, jax.lax.axis_index(comm_axis), local_x.shape[1])
+        met_up = map(lambda p: (p, (p + 1) % value_now), range(value_now))
+        work_now = range(value_now)
+        d_next = map(lambda p: (p, (p - 1) % value_now), work_now)
+        lanes = list(d_next)
+        r2 = jnp.zeros((*local_x.shape[:1], value_now * g_now, *local_x.shape[2:]), local_x.dtype)
+        blocks_here = list(met_up)
+        r2 = lax.dynamic_update_slice_in_dim(r2, local_x, piece_out * g_now, axis=1)
+        r1 = arr_out = local_x
+        answer = value_now // 2
+        for nth in range(1, answer + 1):
+            r1 = jax.lax.ppermute(r1, axis_name=comm_axis, perm=blocks_here)
+            r2 = lax.dynamic_update_slice_in_dim(
+                r2, r1, (piece_out - nth) % value_now * g_now, axis=1
+            )
+            if nth < value_now - answer:
+                arr_out = jax.lax.ppermute(arr_out, axis_name=comm_axis, perm=lanes)
+                r2 = lax.dynamic_update_slice_in_dim(
+                    r2, arr_out, (piece_out + nth) % value_now * g_now, axis=1
+                )
+        return r2
+
     row_block, local_len, width = activations.shape
     row_total = row_block * local_len
     offset = lax.axis_index("group") * local_len
@@ -175,7 +201,7 @@
     hat_two, inverse_two = normalize(middle)
     normed_two = (hat_two * to_float(gain_two) + to_float(shift_two)).astype(jnp.bfloat16)
     fc1_full, fc2_full, bias_fc1 = (
-        lax.all_gather(w_fc1.astype(jnp.bfloat16), "group", axis=1, tiled=True),
+        review_pieces_all_all(w_fc1.astype(jnp.bfloat16)),
         lax.all_gather(w_fc2.astype(jnp.bfloat16), "group", axis=0, tiled=True),
         lax.all_gather(fc1_bias.astype(jnp.bfloat16), "group", axis=0, tiled=True),
     )

time: 942 us -> 918 us (0.975)
  waiting for transfers between devices: 356 us -> 305 us
  blocking collectives: 308 us -> 331 us
    ppermute x0 -> x3, waiting for transfers between devices: none -> 31 us  [the longest x2 31 us: review_pieces_all_all(): r1 = jax.lax.ppermute(r1, axis_name=comm_axis, perm=blocks_here)]
    all_gather x1, waiting for transfers between devices: 28.4 us -> 0.01 us  [per_device(): lax.all_gather(values_new.reshape(row_block, local_len, width), 'group',...]
    all_gather x1 -> x0, waiting for transfers between devices: 25.6 us -> none  [per_device(): lax.all_gather(w_fc1.astype(jnp.bfloat16), 'group', axis=1, tiled=True)]
    all_gather x1, blocking collectives: 5.2 us -> 28.7 us  [per_device(): lax.all_gather(fc1_bias.astype(jnp.bfloat16), 'group', axis=0, tiled=True)]
    all_gather x1, waiting for transfers between devices: 30.4 us -> 13.5 us  [per_device(): lax.all_gather(keys_new.reshape(row_block, local_len, width), 'group', ax...]
    all_gather x1, waiting for transfers between devices: 31.4 us -> 20.7 us  [per_device(): lax.all_gather(w_fc2.astype(jnp.bfloat16), 'group', axis=0, tiled=True)]
  transfers between devices with their start and end apart: 16 -> 18, of which waited for: 13 -> 11; matrix products, arithmetic and copies ran while one was open for 13% -> 14% of each run, Pallas kernels for 0% -> 0%
where the time goes in v1:
time: 918 us; the launch traced here: 911 us
  blocking collectives  331 us (36%)
  waiting for transfers between devices  305 us (33%)
  matrix products  147 us (16%)
  local copies, waits for them, and re-layouts  64.2 us (7%)
  other arithmetic  44.2 us (5%)
  between operations  17 us (2%)
    psum x1, blocking collectives, per_device(): lax.psum((grad_query_full, grad_key_full, grad_value_full, grad_out_full,...  279 us
    reduce_scatter x1, waiting for transfers between devices, per_device(): lax.psum_scatter(grad_fc1.astype(jnp.bfloat16), 'group', scatter_dimensio...  50.4 us
    reduce_scatter x1, waiting for transfers between devices, per_device(): lax.psum_scatter(grad_fc2.astype(jnp.bfloat16), 'group', scatter_dimensio...  50.3 us
    reduce_scatter x1, waiting for transfers between devices, per_device(): lax.psum_scatter(value_parts.astype(jnp.bfloat16), 'group', scatter_dimen...  37.4 us
    ppermute x2, waiting for transfers between devices, review_pieces_all_all(): r1 = jax.lax.ppermute(r1, axis_name=comm_axis, perm=blocks_here)  31 us
    reduce_scatter x1, waiting for transfers between devices, per_device(): lax.psum_scatter(key_parts.astype(jnp.bfloat16), 'group', scatter_dimensi...  29.1 us
    all_gather x1, blocking collectives, per_device(): lax.all_gather(fc1_bias.astype(jnp.bfloat16), 'group', axis=0, tiled=True)  28.7 us
    reduce_scatter x1, waiting for transfers between devices, per_device(): lax.psum_scatter(grad_value_full.astype(jnp.bfloat16), 'group', scatter_d...  27.5 us
  transfers between devices with their start and end apart: 18, of which 11 were waited for; matrix products, arithmetic and copies ran while one was open for 14% of the time, Pallas kernels for 0%

profile of v1, /device:TPU:0, one launch (start us, length us, event | category | flops | bytes accessed | tf_op | source)
XLA Modules:
  0.0 910.6 jit_solution(6277222071585377412)
XLA Ops:
  7.3 1.9 convert_element_type.265
  13.8 13.2 %all-reduce.19 = (bf16[768]{0:T(1024)(128)(2,1)S(1)}, bf16[768]{0:T(1024)(128)(2,1)S(1)}, bf16[768]{0:T(1024)(128)(2,1)S(1)}, bf16[768]{0:T(1024)(128)(2,1)S(1)}...) all-reduce(bf16[768]{0:T(1024)(128)(2,1)S(1)} %dynamic-update-slice, ...), channel_id=1, replica_groups=mesh['group'=4,'replica'=8] {'group'}, use_global_device_ids=true, to_apply=%add.1 | all-reduce | flops 5376 | bytes 21504
  30.6 2.1 add_convert_fusion.3
  33.9 16.3 %all-gather.15.cloned.1.call-done = bf16[768,768]{0,1:T(8,128)(2,1)} async-done(((bf16[768,192]{0,1:T(8,128)(2,1)}), bf16[768,768]{0,1:T(8,128)(2,1)}) %all-gather.15.cloned.1.call-update) | async-done | bytes 1179664 | tf_op jit(solution)/shard_map/all_gather | solution.py:165
  50.2 2.1 convolution_convert_fusion.4
  57.6 1.9 copy-done.19
  61.6 31.0 %collective-permute-done = bf16[768,768]{1,0:T(8,128)(2,1)} collective-permute-done((bf16[768,768]{1,0:T(8,128)(2,1)}, bf16[768,768]{1,0:T(8,128)(2,1)}, u32[]{:S(2)}, u32[]{:S(2)}) %collective-permute-start) | collective-permute-done | bytes 1179680 | tf_op jit(solution)/shard_map/ppermute | solution.py:135
  93.8 28.7 %all-gather = bf16[4,1,768]{2,1,0:T(2,128)(2,1)S(1)} all-gather(bf16[1,1,768]{2,1,0:T(2,128)(2,1)S(1)} %reshape.383), channel_id=1, replica_groups=mesh['group'=4,'replica'=8] {'group'}, dimensions={0}, use_global_device_ids=true | all-gather | bytes 7680 | tf_op jit(solution)/shard_map/all_gather | solution.py:206
  124.2 2.6 constant_dynamic-update-slice_fusion.6
  126.8 2.6 constant_dynamic-update-slice_fusion.5
  129.4 2.1 add_convert_fusion.2
  131.8 2.4 constant_dynamic-update-slice_fusion.4
  134.2 13.5 %all-gather.17.cloned.1.call-done = bf16[2,1024,768]{1,2,0:T(8,128)(2,1)} async-done(((bf16[2,256,768]{1,2,0:T(8,128)(2,1)}), bf16[2,1024,768]{1,2,0:T(8,128)(2,1)}) %all-gather.17.cloned.1.call-update) | async-done | bytes 3145744 | tf_op jit(solution)/shard_map/all_gather | solution.py:190
  147.6 29.5 %while.26 = (s32[]{:T(128)}, bf16[2,256,768]{2,1,0:T(8,128)(2,1)}, f32[2,12,256]{2,1,0:T(8,128)}, bf16[2,1024,768]{1,2,0:T(8,128)(2,1)}, s32[2,256]{1,0:T(2,128)...) while((s32[]{:T(128)}, bf16[2,256,768]{2,1,0:T(8,128)(2,1)}, ...), condition=%wide.region_5.6_spmd, body=%wide.region_2.5_spmd.sunk | while | flops 843510784 | bytes 51499116 | solution.py:196
  148.7 2.2 constant_dynamic-slice_fusion.23
  151.0 2.3 fusion.100
  153.3 3.6 fusion.101
  157.6 3.9 fusion.102
  163.4 2.2 constant_dynamic-slice_fusion.23
  165.7 2.3 fusion.100
  168.0 3.6 fusion.101
  172.2 3.9 fusion.102
  177.1 2.8 fusion.32
  181.1 4.9 fusion.28
  186.1 20.7 %all-gather.21.cloned.1.call-done = bf16[3072,768]{1,0:T(8,128)(2,1)} async-done(((bf16[768,768]{1,0:T(8,128)(2,1)}), bf16[3072,768]{1,0:T(8,128)(2,1)}) %all-gather.21.cloned.1.call-update) | async-done | bytes 4718608 | tf_op jit(solution)/shard_map/all_gather | solution.py:205
  206.8 9.7 %fusion.29 = (bf16[3072]{0:T(1024)(128)(2,1)}, bf16[512,3072]{1,0:T(8,128)(2,1)S(1)}) fusion(f32[512,3072]{1,0:T(8,128)} %fusion.28, f32[3072]{0:T(1024)S(1)} %bitcast.214, bf16[512,768]{1,0:T(8,128)(2,1)S(1)} %copy-done.26, bf16[3072,768]{1,0:T(8,128)(2,1)} %all-gather.21.cloned.1.call-done), kind=kOutput, calls=%fused_computation.112 | convolution fusion | flops 2450519040 | bytes 14960640 | tf_op jit(solution)/shard_map/dot_general | solution.py:217
  216.6 3.5 multiply_reduce_fusion.1
  222.5 108.3 %while.27 = (s32[]{:T(128)}, bf16[2,256,768]{1,2,0:T(8,128)(2,1)}, bf16[2,1024,768]{2,1,0:T(8,128)(2,1)}, bf16[2,1024,768]{2,1,0:T(8,128)(2,1)}, bf16[2,1024,768...) while((s32[]{:T(128)}, bf16[2,256,768]{1,2,0:T(8,128)(2,1)}, ...), condition=%wide.region_12.13_spmd, body=%wide.region_10.12_spmd.sunk | while | flops 2062676992 | bytes 238113392 | solution.py:244
  223.0 2.1 constant_dynamic-slice_fusion.27
  225.1 6.4 fusion.113
  234.5 11.5 %multiply_reduce_fusion.10 = (f32[12,256]{1,0:T(8,128)S(1)}, f32[12,256,1024]{2,1,0:T(8,128)}) fusion(f32[12,256,1024]{2,1,0:T(8,128)} %fusion.113, f32[12,256]{1,0:T(8,128)S(1)} %dynamic-slice_bitcast_fusion.2, pred[256,1024]{1,0:T(8,128)(4,1)S(1)} %broadcast_compare_fusion.5, bf16[256,12,64]{0,2,1:T(8,128)(2,1)S(1)} %bitcast.188, ...), kind=kOutput, calls=%fused_computation.18.clone.1 | convolution fusion | flops 418378752 | bytes 27418624 | tf_op jit(solution)/shard_map/while/body/eval_jaxpr/qhe,khe->hqk/dot_general | solution.py:73
  247.1 6.7 multiply_convert_fusion.6
  257.9 9.0 fusion.115
  267.0 2.7 copy.97
  269.7 3.4 constant_dynamic-update-slice_fusion.13
  274.1 2.0 fusion.114
  276.9 2.1 constant_dynamic-slice_fusion.27
  279.1 6.4 fusion.113
  288.4 11.5 %multiply_reduce_fusion.10 = (f32[12,256]{1,0:T(8,128)S(1)}, f32[12,256,1024]{2,1,0:T(8,128)}) fusion(f32[12,256,1024]{2,1,0:T(8,128)} %fusion.113, f32[12,256]{1,0:T(8,128)S(1)} %dynamic-slice_bitcast_fusion.2, pred[256,1024]{1,0:T(8,128)(4,1)S(1)} %broadcast_compare_fusion.5, bf16[256,12,64]{0,2,1:T(8,128)(2,1)S(1)} %bitcast.188, ...), kind=kOutput, calls=%fused_computation.18.clone.1 | convolution fusion | flops 418378752 | bytes 27418624 | tf_op jit(solution)/shard_map/while/body/eval_jaxpr/qhe,khe->hqk/dot_general | solution.py:73
  301.0 6.7 multiply_convert_fusion.6
  311.9 9.0 fusion.115
  320.9 2.7 copy.97
  323.6 3.4 constant_dynamic-update-slice_fusion.13
  328.0 2.0 fusion.114
  333.7 3.0 bitcast_convert_fusion.2
  336.9 3.0 convolution_convert_fusion.2
  339.9 29.1 %reduce-scatter.9.cloned.1.call-done = bf16[2,256,768]{2,1,0:T(8,128)(2,1)} async-done(((bf16[2,1024,768]{2,1,0:T(8,128)(2,1)}), bf16[2,256,768]{2,1,0:T(8,128)(2,1)}) %reduce-scatter.9.cloned.1.call-update) | async-done | bytes 786448 | tf_op jit(solution)/shard_map/reduce_scatter | solution.py:248
  369.0 3.2 bitcast_convert_fusion.1
  372.3 37.4 %reduce-scatter.11.cloned.1.call-done = bf16[2,256,768]{2,1,0:T(8,128)(2,1)} async-done(((bf16[2,1024,768]{2,1,0:T(8,128)(2,1)}), bf16[2,256,768]{2,1,0:T(8,128)(2,1)}) %reduce-scatter.11.cloned.1.call-update) | async-done | bytes 786448 | tf_op jit(solution)/shard_map/reduce_scatter | solution.py:251
  409.7 3.2 bitcast_convert_fusion
  413.0 8.9 convolution_convert_fusion
  422.5 7.4 convolution_convert_fusion.1
  433.8 2.3 copy.57
  437.4 3.5 fusion.34
  440.9 26.1 %reduce-scatter.19.cloned.1.call-done = bf16[192,768]{1,0:T(8,128)(2,1)} async-done(((bf16[768,768]{1,0:T(8,128)(2,1)}), bf16[192,768]{1,0:T(8,128)(2,1)}) %reduce-scatter.19.cloned.1.call-update) | async-done | bytes 294928 | tf_op jit(solution)/shard_map/reduce_scatter | solution.py:296
  468.3 2.4 fusion.35
  470.8 2.4 multiply_reduce_fusion.2
  473.3 10.3 %all-reduce.18 = (bf16[768]{0:T(1024)(128)(2,1)S(1)}, bf16[768]{0:T(1024)(128)(2,1)S(1)}, bf16[768]{0:T(1024)(128)(2,1)S(1)}, bf16[768]{0:T(1024)(128)(2,1)S(1)}...) all-reduce(bf16[768]{0:T(1024)(128)(2,1)S(1)} %dynamic-update-slice, ...), channel_id=1, replica_groups=mesh['group'=4,'replica'=8] {'group'}, use_global_device_ids=true, to_apply=%add.7 | all-reduce | flops 9984 | bytes 39936
  484.2 3.2 multiply_add_fusion
  487.4 9.3 %add_add_fusion.1 = f32[512,768]{1,0:T(8,128)} fusion(f32[512,768]{1,0:T(8,128)S(1)} %copy-done.16, bf16[3072,768]{1,0:T(8,128)(2,1)} %all-gather.21.cloned.1.call-done, f32[768]{0:T(1024)S(1)} %convert_element_type.289, f32[512,3072]{1,0:T(8,128)} %fusion.28, f32[3072]{0:T(1024)S(1)} %bitcast.216), kind=kOutput, calls=%fused_computation.67 | convolution fusion | flops 2432434176 | bytes 14171136 | tf_op jit(solution)/shard_map/dot_general | solution.py:211
  496.7 27.5 %reduce-scatter.17.cloned.1.call-done = bf16[768,192]{0,1:T(8,128)(2,1)} async-done(((bf16[768,768]{0,1:T(8,128)(2,1)}), bf16[768,192]{0,1:T(8,128)(2,1)}) %reduce-scatter.17.cloned.1.call-update) | async-done | bytes 294928 | tf_op jit(solution)/shard_map/reduce_scatter | solution.py:293
  524.2 50.3 %reduce-scatter.23.cloned.1.call-done = bf16[768,768]{1,0:T(8,128)(2,1)} async-done(((bf16[3072,768]{1,0:T(8,128)(2,1)}), bf16[768,768]{1,0:T(8,128)(2,1)}) %reduce-scatter.23.cloned.1.call-update) | async-done | bytes 1179664 | tf_op jit(solution)/shard_map/reduce_scatter | solution.py:227
  574.4 50.4 %reduce-scatter.21.cloned.1.call-done = bf16[768,768]{1,0:T(8,128)(2,1)} async-done(((bf16[768,3072]{1,0:T(8,128)(2,1)}), bf16[768,768]{1,0:T(8,128)(2,1)}) %reduce-scatter.21.cloned.1.call-update) | async-done | bytes 1179664 | tf_op jit(solution)/shard_map/reduce_scatter | solution.py:224
  624.9 279.0 %all-reduce.21 = (f32[192]{0:T(256)}, f32[192]{0:T(256)}, f32[768,192]{0,1:T(8,128)}, f32[192]{0:T(256)}, f32[768,192]{0,1:T(8,128)}, /*index=5*/f32[768,192]{0,...) all-reduce(f32[192]{0:T(256)S(1)} %dynamic-slice_convert_fusion.8, ...), channel_id=1, replica_groups=mesh['group'=4,'replica'=8] {'replica'}, use_global_device_ids=true, to_apply=%region_19.20 | all-reduce | flops 1771776 | bytes 10635264 | tf_op jit(solution)/shard_map/psum | solution.py:340
  (361 shorter events, 56.8 us)
Async XLA Ops:
  7.2 3.7 copy-start.70
  7.2 3.8 copy-start.71
  7.2 3.8 copy-start.72
  7.2 3.8 copy-start.73
  7.3 3.8 copy-start.74
  7.3 3.8 copy-start.75
  7.3 3.8 copy-start.76
  7.3 23.3 %all-gather.9.cloned.1.call-start = ((), (), s32[]{:S(2)}) async-start(), calls=%async_computation.8 | async-start | bytes 1474560 | tf_op jit(solution)/shard_map/all_gather | solution.py:166
  9.2 17.8 %copy-start.5 = (f32[2,256,768]{2,1,0:T(8,128)S(1)}, f32[2,256,768]{2,1,0:T(8,128)}, u32[]{:S(2)}) copy-start(f32[2,256,768]{2,1,0:T(8,128)} %param.22) | copy-start | bytes 4718596
  9.2 41.0 %all-gather.15.cloned.1.call-start = ((), (), s32[]{:S(2)}) async-start(), calls=%async_computation.11 | async-start | bytes 1474560 | tf_op jit(solution)/shard_map/all_gather | solution.py:165
  10.1 119.3 %all-gather.13.cloned.1.call-start = ((), (), s32[]{:S(2)}) async-start(), calls=%async_computation.10 | async-start | bytes 1474560 | tf_op jit(solution)/shard_map/all_gather | solution.py:164
  10.9 123.3 %all-gather.11.cloned.1.call-start = ((), (), s32[]{:S(2)}) async-start(), calls=%async_computation.9 | async-start | bytes 3932160 | tf_op jit(solution)/shard_map/all_gather | solution.py:191
  28.7 21.5 %copy-start.27 = (bf16[512,768]{1,0:T(8,128)(2,1)}, bf16[512,768]{1,0:T(8,128)(2,1)S(1)}, u32[]{:S(2)}) copy-start(bf16[512,768]{1,0:T(8,128)(2,1)S(1)} %add_convert_fusion.4) | copy-start | bytes 2359300
  33.8 113.8 %all-gather.17.cloned.1.call-start = ((), (), s32[]{:S(2)}) async-start(), calls=%async_computation.12 | async-start | bytes 3932160 | tf_op jit(solution)/shard_map/all_gather | solution.py:190
  53.5 123.6 %all-gather.19.cloned.1.call-start = ((), (), s32[]{:S(2)}) async-start(), calls=%async_computation.13 | async-start | bytes 1474560 | tf_op jit(solution)/shard_map/all_gather | solution.py:167
  54.3 152.5 %all-gather.21.cloned.1.call-start = ((), (), s32[]{:S(2)}) async-start(), calls=%async_computation.14 | async-start | bytes 5898240 | tf_op jit(solution)/shard_map/all_gather | solution.py:205
  56.1 3.6 copy-start.23
  57.3 36.5 %copy-start.62 = (f32[768]{0:T(1024)S(1)}, f32[768]{0:T(1024)}, u32[]{:S(2)}) copy-start(f32[768]{0:T(1024)} %param.37) | copy-start | bytes 9220
  57.3 35.2 %collective-permute-start = (bf16[768,768]{1,0:T(8,128)(2,1)}, bf16[768,768]{1,0:T(8,128)(2,1)}, u32[]{:S(2)}, u32[]{:S(2)}) collective-permute-start(bf16[768,768]{1,0:T(8,128)(2,1)} %get-tuple-element.266), channel_id=1, source_target_pairs={{0,8},{8,16},{16,24},{24,0},{1,9},{9,17},{17,25},{25,1},{2,10},{10... | collective-permute-start | bytes 3538952 | tf_op jit(solution)/shard_map/ppermute | solution.py:135
  59.5 67.3 %collective-permute-start.1 = (bf16[768,768]{1,0:T(8,128)(2,1)}, bf16[768,768]{1,0:T(8,128)(2,1)}, u32[]{:S(2)}, u32[]{:S(2)}) collective-permute-start(bf16[768,768]{1,0:T(8,128)(2,1)} %get-tuple-element.266), channel_id=1, source_target_pairs={{0,24},{8,0},{16,8},{24,16},{1,25},{9,1},{17,9},{25,17},{2,26},{10... | collective-permute-start | bytes 3538952 | tf_op jit(solution)/shard_map/ppermute | solution.py:140
  59.7 63.5 %copy-start.12 = (f32[2,256,768]{2,1,0:T(8,128)S(1)}, f32[2,256,768]{2,1,0:T(8,128)}, u32[]{:S(2)}) copy-start(f32[2,256,768]{2,1,0:T(8,128)} %param.23) | copy-start | bytes 4718596
  60.8 308.2 %reduce-scatter.9.cloned.1.call-start = ((), (), s32[]{:S(2)}) async-start(), calls=%async_computation.15 | async-start | bytes 3932160 | tf_op jit(solution)/shard_map/reduce_scatter | solution.py:248
  61.6 158.6 %copy-start.52 = (f32[768]{0:T(1024)}, f32[768]{0:T(1024)S(1)}, u32[]{:S(2)}) copy-start(f32[768]{0:T(1024)S(1)} %convert_element_type.279) | copy-start | bytes 9220
  61.6 118.7 %copy-start.63 = (f32[768]{0:T(1024)}, f32[768]{0:T(1024)S(1)}, u32[]{:S(2)}) copy-start(f32[768]{0:T(1024)S(1)} %convert_element_type.281) | copy-start | bytes 9220
  92.5 39.2 %collective-permute-start.2 = (bf16[768,768]{1,0:T(8,128)(2,1)}, bf16[768,768]{1,0:T(8,128)(2,1)}, u32[]{:S(2)}, u32[]{:S(2)}) collective-permute-start(bf16[768,768]{1,0:T(8,128)(2,1)} %collective-permute-done), channel_id=1, source_target_pairs={{0,8},{8,16},{16,24},{24,0},{1,9},{9,17},{17,25},{25,1},{2,10},{10... | collective-permute-start | bytes 3538952 | tf_op jit(solution)/shard_map/ppermute | solution.py:135
  93.8 33.0 %copy-start.50 = (f32[1,2,2,128]{3,1,2,0:T(2,128)}, f32[1,2,2,128]{3,1,2,0:T(2,128)S(1)}, u32[]{:S(2)}) copy-start(f32[1,2,2,128]{3,1,2,0:T(2,128)S(1)} %copy.90) | copy-start | bytes 6148
  177.1 4.0 copy-start.20
  180.0 40.1 %copy-start.48 = (f32[512]{0:T(512)}, f32[512]{0:T(512)S(1)}, u32[]{:S(2)}) copy-start(f32[512]{0:T(512)S(1)} %broadcast_multiply_fusion.4) | copy-start | bytes 6148
  181.1 39.0 %copy-start.59 = (f32[512]{0:T(512)}, f32[512]{0:T(512)S(1)}, u32[]{:S(2)}) copy-start(f32[512]{0:T(512)S(1)} %add_rsqrt_fusion) | copy-start | bytes 6148
  181.1 25.7 %copy-start.26 = (bf16[512,768]{1,0:T(8,128)(2,1)S(1)}, bf16[512,768]{1,0:T(8,128)(2,1)}, u32[]{:S(2)}) copy-start(bf16[512,768]{1,0:T(8,128)(2,1)} %fusion.21) | copy-start | bytes 2359300
  181.1 25.7 %copy-start.54 = (f32[4,1,768]{2,1,0:T(1,128)S(1)}, f32[4,1,768]{2,1,0:T(1,128)}, u32[]{:S(2)}) copy-start(f32[4,1,768]{2,1,0:T(1,128)} %convert_element_type.326) | copy-start | bytes 36868
  181.1 35.4 %slice-start.3 = ((s8[4718592]{0:T(1024)(128)(4,1)}), s8[524288]{0:T(1024)(128)(4,1)S(1)}, s32[]{:S(2)}) async-start(s8[4718592]{0:T(1024)(128)(4,1)} %bitcast.192), calls=%async_computation.26 | async-start | bytes 1048576
  206.8 9.7 %copy-start.15 = (f32[512,768]{1,0:T(8,128)S(1)}, f32[512,768]{1,0:T(8,128)}, u32[]{:S(2)}) copy-start(f32[512,768]{1,0:T(8,128)} %copy-done.14) | copy-start | bytes 4718596
  206.8 9.7 %slice-start.4 = ((s8[4718592]{0:T(1024)(128)(4,1)}), s8[4194304]{0:T(1024)(128)(4,1)S(1)}, s32[]{:S(2)}) async-start(s8[4718592]{0:T(1024)(128)(4,1)} %bitcast.192), calls=%async_computation.27 | async-start | bytes 8388608
  216.5 3.6 copy-start.78
  216.6 3.6 copy-start.13
  216.6 3.6 copy-start.51
  222.9 9.3 %copy-start.38 = (s32[2,256]{1,0:T(2,128)}, s32[2,256]{1,0:T(2,128)S(1)}, u32[]{:S(2)}) copy-start(s32[2,256]{1,0:T(2,128)S(1)} %get-tuple-element.475) | copy-start | bytes 6148 | tf_op jit(solution)/shard_map/while
  223.0 9.5 %copy-start.17 = (bf16[2,256,768]{2,1,0:T(8,128)(2,1)}, bf16[2,256,768]{2,1,0:T(8,128)(2,1)S(1)}, u32[]{:S(2)}) copy-start(bf16[2,256,768]{2,1,0:T(8,128)(2,1)S(1)} %get-tuple-element.479) | copy-start | bytes 2359300 | tf_op jit(solution)/shard_map/while
  225.1 7.4 copy-start.35
  232.5 13.5 %copy-start.3 = (pred[256,1024]{1,0:T(8,128)(4,1)}, pred[256,1024]{1,0:T(8,128)(4,1)S(1)}, u32[]{:S(2)}) copy-start(pred[256,1024]{1,0:T(8,128)(4,1)S(1)} %broadcast_compare_fusion.5) | copy-start | bytes 786436 | tf_op jit(solution)/shard_map/while
  234.4 11.6 %slice-start = ((s8[12582912]{0:T(1024)(128)(4,1)}), s8[4194304]{0:T(1024)(128)(4,1)S(1)}, s32[]{:S(2)}) async-start(s8[12582912]{0:T(1024)(128)(4,1)} %bitcast.175), calls=%async_computation.23 | async-start | bytes 8388608 | tf_op jit(solution)/shard_map/while
  234.4 11.6 %slice-start.1 = ((s8[12582912]{0:T(1024)(128)(4,1)}), s8[4194304]{0:T(1024)(128)(4,1)S(1)}, s32[]{:S(2)}) async-start(s8[12582912]{0:T(1024)(128)(4,1)} %bitcast.175), calls=%async_computation.24 | async-start | bytes 8388608 | tf_op jit(solution)/shard_map/while
  234.4 12.6 %slice-start.2 = ((s8[12582912]{0:T(1024)(128)(4,1)}), s8[4194304]{0:T(1024)(128)(4,1)S(1)}, s32[]{:S(2)}) async-start(s8[12582912]{0:T(1024)(128)(4,1)} %bitcast.175), calls=%async_computation.25 | async-start | bytes 8388608 | tf_op jit(solution)/shard_map/while
  269.7 4.4 copy-start.1
  276.9 9.3 %copy-start.38 = (s32[2,256]{1,0:T(2,128)}, s32[2,256]{1,0:T(2,128)S(1)}, u32[]{:S(2)}) copy-start(s32[2,256]{1,0:T(2,128)S(1)} %get-tuple-element.475) | copy-start | bytes 6148 | tf_op jit(solution)/shard_map/while
  276.9 9.6 %copy-start.17 = (bf16[2,256,768]{2,1,0:T(8,128)(2,1)}, bf16[2,256,768]{2,1,0:T(8,128)(2,1)S(1)}, u32[]{:S(2)}) copy-start(bf16[2,256,768]{2,1,0:T(8,128)(2,1)S(1)} %get-tuple-element.479) | copy-start | bytes 2359300 | tf_op jit(solution)/shard_map/while
  279.1 7.4 copy-start.35
  286.4 13.5 %copy-start.3 = (pred[256,1024]{1,0:T(8,128)(4,1)}, pred[256,1024]{1,0:T(8,128)(4,1)S(1)}, u32[]{:S(2)}) copy-start(pred[256,1024]{1,0:T(8,128)(4,1)S(1)} %broadcast_compare_fusion.5) | copy-start | bytes 786436 | tf_op jit(solution)/shard_map/while
  288.4 11.6 %slice-start = ((s8[12582912]{0:T(1024)(128)(4,1)}), s8[4194304]{0:T(1024)(128)(4,1)S(1)}, s32[]{:S(2)}) async-start(s8[12582912]{0:T(1024)(128)(4,1)} %bitcast.175), calls=%async_computation.23 | async-start | bytes 8388608 | tf_op jit(solution)/shard_map/while
  288.4 11.6 %slice-start.1 = ((s8[12582912]{0:T(1024)(128)(4,1)}), s8[4194304]{0:T(1024)(128)(4,1)S(1)}, s32[]{:S(2)}) async-start(s8[12582912]{0:T(1024)(128)(4,1)} %bitcast.175), calls=%async_computation.24 | async-start | bytes 8388608 | tf_op jit(solution)/shard_map/while
  288.4 12.6 %slice-start.2 = ((s8[12582912]{0:T(1024)(128)(4,1)}), s8[4194304]{0:T(1024)(128)(4,1)S(1)}, s32[]{:S(2)}) async-start(s8[12582912]{0:T(1024)(128)(4,1)} %bitcast.175), calls=%async_computation.25 | async-start | bytes 8388608 | tf_op jit(solution)/shard_map/while
  323.6 4.4 copy-start.1
  330.9 78.8 %reduce-scatter.11.cloned.1.call-start = ((), (), s32[]{:S(2)}) async-start(), calls=%async_computation.16 | async-start | bytes 3932160 | tf_op jit(solution)/shard_map/reduce_scatter | solution.py:251
  331.6 109.3 %reduce-scatter.13.cloned.1.call-start = ((), (), s32[]{:S(2)}) async-start(), calls=%async_computation.17 | async-start | bytes 1474560 | tf_op jit(solution)/shard_map/reduce_scatter | solution.py:287
  336.8 130.1 %reduce-scatter.19.cloned.1.call-start = ((), (), s32[]{:S(2)}) async-start(), calls=%async_computation.20 | async-start | bytes 1474560 | tf_op jit(solution)/shard_map/reduce_scatter | solution.py:296
  339.9 156.8 %reduce-scatter.15.cloned.1.call-start = ((), (), s32[]{:S(2)}) async-start(), calls=%async_computation.18 | async-start | bytes 1474560 | tf_op jit(solution)/shard_map/reduce_scatter | solution.py:290
  372.2 40.7 %copy-start.55 = (f32[4,1,768]{2,1,0:T(1,128)S(1)}, f32[4,1,768]{2,1,0:T(1,128)}, u32[]{:S(2)}) copy-start(f32[4,1,768]{2,1,0:T(1,128)} %convert_element_type.326) | copy-start | bytes 36868
  372.2 151.9 %reduce-scatter.17.cloned.1.call-start = ((), (), s32[]{:S(2)}) async-start(), calls=%async_computation.19 | async-start | bytes 1474560 | tf_op jit(solution)/shard_map/reduce_scatter | solution.py:293
  412.9 161.5 %reduce-scatter.23.cloned.1.call-start = ((), (), s32[]{:S(2)}) async-start(), calls=%async_computation.22 | async-start | bytes 5898240 | tf_op jit(solution)/shard_map/reduce_scatter | solution.py:227
  421.9 203.0 %reduce-scatter.21.cloned.1.call-start = ((), (), s32[]{:S(2)}) async-start(), calls=%async_computation.21 | async-start | bytes 5898240 | tf_op jit(solution)/shard_map/reduce_scatter | solution.py:224
  484.2 3.2 copy-start.16
  487.4 137.5 %copy-start.33 = (bf16[768,192]{0,1:T(8,128)(2,1)S(1)}, bf16[768,192]{0,1:T(8,128)(2,1)}, u32[]{:S(2)}) copy-start(bf16[768,192]{0,1:T(8,128)(2,1)} %reduce-scatter.13.cloned.1.call-done) | copy-start | bytes 884740
  487.4 137.5 %copy-start.34 = (bf16[192,768]{1,0:T(8,128)(2,1)S(1)}, bf16[192,768]{1,0:T(8,128)(2,1)}, u32[]{:S(2)}) copy-start(bf16[192,768]{1,0:T(8,128)(2,1)} %reduce-scatter.19.cloned.1.call-done) | copy-start | bytes 884740
  (54 other events, 102.5 us)
Sparse Core Ops, SparseCore 0:
  10.3 20.2 all-gather.8
  32.7 17.4 all-gather.14
  52.3 23.6 all-gather.12
  78.0 39.2 all-gather.10
  118.7 28.9 all-gather.16
  149.6 17.4 all-gather.18
  169.3 37.4 all-gather.20
  331.0 37.9 reduce-scatter.8
  371.7 37.9 reduce-scatter.10
  412.7 25.7 reduce-scatter.12
  441.2 25.7 reduce-scatter.18
  469.9 25.7 reduce-scatter.14
  498.4 25.7 reduce-scatter.16
  526.6 47.8 reduce-scatter.22
  577.0 47.8 reduce-scatter.20
